TPU v7x, 32 devices: a whole 2x2x4 slice. The times are simulated.
32 devices in a mesh: ia: 2 (over x), ja: 4 (over y, core), ka: 4 (over z).
Axes of the slice: x: 2, y: 2, z: 4, core: 2. Of those that a mesh axis runs over, the one named last changes fastest.
Arguments:
- tensor: bfloat16 [512, 512, 512], P('ia', 'ja', 'ka'), may hold values from 0 to 122880
- matrix: bfloat16 [512, 32768], P(None, ('ia', 'ja', 'ka')), may hold values from 0 to 4096000
- first_factor: bfloat16 [512, 256], P('ia'), may hold values from 0.05 to 2
- second_factor: bfloat16 [512, 256], P('ja'), may hold values from 0.05 to 2
- time_factor: bfloat16 [512, 256], P('ka'), may hold values from 0.05 to 2
- column_factor: bfloat16 [32768, 256], P(('ia', 'ja', 'ka')), may hold values from 0.05 to 2
Outputs:
- first_new: bfloat16 [512, 256], P('ia')
- second_new: bfloat16 [512, 256], P('ja')
- time_new: bfloat16 [512, 256], P('ka')
All inputs are finite; a program needn't handle non-finite values.
Results may differ from a plain program's by a relative error of at most 0.00075.
The roundings to bfloat16 on the way count: a program that leaves them out, or rounds other values in their place, can miss the bound.
Values may be sent and summed in bfloat16 or wider, within the bound.
No kernel may reach another device: no remote copies, remote signals or barrier semaphores. Data moves between devices by JAX's collectives and lax.ppermute only.
A program may use at most 128 MiB of HBM per device.

v0:
```python
import jax
import jax.numpy as jnp
from jax import lax
from jax.sharding import PartitionSpec as P


def cross_product(values):
    return jnp.dot(values.T, values, preferred_element_type=jnp.float32)


def rescale(factor, numerator, gram_total):
    widened = factor.astype(jnp.float32)
    denominator = jnp.dot(widened, gram_total, precision=lax.Precision.HIGHEST)
    return (widened * numerator / denominator).astype(jnp.bfloat16)


def on_device(tensor, matrix, first_factor, second_factor, time_factor, column_factor):
    first_rows = lax.axis_index("ia") == 0
    first_plane = lax.axis_index("ja") == 0
    first_time = lax.axis_index("ka") == 0
    gram_second = jnp.where(first_rows & first_time, cross_product(second_factor), 0.0)
    gram_time = jnp.where(first_rows & first_plane, cross_product(time_factor), 0.0)
    gram_column = cross_product(column_factor)
    gram_second, gram_time, gram_column = lax.psum(
        (gram_second, gram_time, gram_column), ("ia", "ja", "ka")
    )
    gram_total = gram_second * gram_time + gram_column
    tile_i, tile_j, tile_k = tensor.shape
    rank_size = first_factor.shape[1]
    khatri = (
        (
            second_factor.astype(jnp.float32)[:, None, :]
            * time_factor.astype(jnp.float32)[None, :, :]
        )
        .astype(jnp.bfloat16)
        .reshape(tile_j * tile_k, rank_size)
    )
    slab = jnp.dot(
        tensor.reshape(tile_i, tile_j * tile_k), khatri, preferred_element_type=jnp.float32
    )
    coupled = jnp.dot(matrix, column_factor, preferred_element_type=jnp.float32)
    offset = lax.axis_index("ia") * tile_i
    coupled = lax.psum(coupled, ("ia", "ja", "ka"))
    slab = lax.psum(slab, ("ja", "ka"))
    numerator = slab + lax.dynamic_slice_in_dim(coupled, offset, tile_i, 0)
    first_new = rescale(first_factor, numerator, gram_total)
    weighted = lax.dot_general(
        tensor, first_new, (((0,), (0,)), ((), ())), preferred_element_type=jnp.float32
    )
    plane_sum = jnp.sum(weighted * time_factor.astype(jnp.float32)[None, :, :], axis=1)
    gram_first = jnp.where(first_time, cross_product(first_new), 0.0)
    plane_sum, gram_first = lax.psum((plane_sum, gram_first), ("ia", "ka"))
    second_new = rescale(second_factor, plane_sum, gram_first * gram_time)
    time_sum = jnp.sum(weighted * second_new.astype(jnp.float32)[:, None, :], axis=0)
    gram_new = jnp.where(first_rows, cross_product(second_new), 0.0)
    time_sum, gram_new = lax.psum((time_sum, gram_new), ("ia", "ja"))
    time_new = rescale(time_factor, time_sum, gram_first * gram_new)
    return (first_new, second_new, time_new)


def solution(mesh):
    return jax.shard_map(
        on_device,
        mesh=mesh,
        in_specs=(
            P("ia", "ja", "ka"),
            P(None, ("ia", "ja", "ka")),
            P("ia", None),
            P("ja", None),
            P("ka", None),
            P(("ia", "ja", "ka"), None),
        ),
        out_specs=(P("ia", None), P("ja", None), P("ka", None)),
        check_vma=False,
    )
```

profile of v0, /device:TPU:0, one launch (start us, length us, event | category | flops | bytes accessed | tf_op | source)
XLA Modules:
  0.0 419.7 jit_solution(8857170066738423173)
XLA Ops:
  7.2 1.0 copy.26
  8.3 0.1 copy.27
  8.4 13.1 %copy.32 = bf16[256,128,128]{0,2,1:T(8,128)(2,1)} copy(bf16[256,128,128]{2,1,0:T(8,128)(2,1)} %param.6) | data formatting | bytes 16777216 | tf_op args[0]
  21.8 6.5 %fusion.4 = f32[256,256]{0,1:T(8,128)} fusion(bf16[256,128,128]{0,2,1:T(8,128)(2,1)} %copy.32, f32[128,256]{1,0:T(8,128)S(1)} %copy.27, f32[128,256]{1,0:T(8,128)S(1)} %copy.25), kind=kOutput, calls=%fused_computation.12 | convolution fusion | flops 2155872256 | bytes 8912896 | tf_op jit(solution)/shard_map/dot_general | solution.py:38
  28.3 0.9 convolution_select_fusion.3
  29.3 1.0 fusion.15
  30.3 1.3 fusion.14
  31.6 0.9 convolution_select_fusion.2
  32.7 88.2 %all-reduce.8.cloned.1.call-done = f32[256,256]{0,1:T(8,128)} async-done(((f32[256,256]{0,1:T(8,128)}), f32[256,256]{0,1:T(8,128)}) %all-reduce.8.cloned.1.call-update) | async-done | bytes 262160 | tf_op jit(solution)/shard_map/psum | solution.py:44
  120.9 139.3 %all-reduce.10.cloned.1.call-done = (f32[256,256]{1,0:T(8,128)}, f32[256,256]{1,0:T(8,128)}, f32[256,256]{1,0:T(8,128)}, f32[512,256]{0,1:T(8,128)}) async-done(((f32[256,256]{1,0:T(8,128)}, f32[256,256]{1,0:T(8,128)}, f32[256,256]{1,0:T(8,128)}, f32[512,256]{0,1:T(8,128)}), (f32[256,256]{1,0:T(8,128)}, f32[256,256]{1,0:T(8,128)}, f32[256,256]{1,0:T(8,128)}, ...) | async-done | bytes 1310736 | tf_op jit(solution)/shard_map/psum | solution.py:24
  260.2 1.7 fusion.5
  261.9 0.9 convolution_select_fusion.1
  262.8 11.5 %multiply_reduce_fusion.1 = (f32[128,256]{1,0:T(8,128)S(1)}, f32[256,16384]{0,1}) fusion(f32[128,256]{1,0:T(8,128)S(1)} %copy.27, bf16[256,256]{0,1:T(8,128)(2,1)S(1)} %fusion.5, bf16[256,16384]{0,1:T(8,128)(2,1)} %bitcast.46), kind=kOutput, calls=%fused_computation.1 | convolution fusion | flops 2155839488 | bytes 25559040
  274.3 0.8 copy.33
  275.1 71.3 %all-reduce.12.cloned.1.call-done = (f32[256,256]{1,0:T(8,128)}, f32[128,256]{0,1:T(8,128)}) async-done(((f32[256,256]{1,0:T(8,128)}, f32[128,256]{0,1:T(8,128)}), (f32[256,256]{1,0:T(8,128)}, f32[128,256]{0,1:T(8,128)})) %all-reduce.12.cloned.1.call-update) | async-done | bytes 393232 | tf_op jit(solution)/shard_map/psum | solution.py:52
  346.4 1.4 fusion.9
  348.0 0.9 convolution_select_fusion
  348.9 7.6 %multiply_reduce_fusion = f32[128,256]{1,0:T(8,128)S(1)} fusion(f32[128,128,256]{2,1,0:T(8,128)} %bitcast.45, f32[128,256]{1,0:T(8,128)S(1)} %copy.34), kind=kLoop, calls=%fused_computation | loop fusion | flops 8355840 | bytes 17039360 | tf_op jit(solution)/shard_map/reduce_sum | solution.py:54
  356.5 0.8 copy.35
  357.3 0.8 copy.36
  358.0 0.7 copy.37
  358.8 52.2 %all-reduce.14.cloned.1.call-done = (f32[256,256]{1,0:T(8,128)}, f32[128,256]{0,1:T(8,128)}) async-done(((f32[256,256]{1,0:T(8,128)}, f32[128,256]{0,1:T(8,128)}), (f32[256,256]{1,0:T(8,128)}, f32[128,256]{0,1:T(8,128)})) %all-reduce.14.cloned.1.call-update) | async-done | bytes 393232 | tf_op jit(solution)/shard_map/psum | solution.py:56
  411.0 1.4 fusion.8
  412.4 0.7 copy.38
  (26 shorter events, 0.7 us)
Async XLA Ops:
  7.2 23.1 %copy-start = (bf16[512,1024]{1,0:T(8,128)(2,1)S(1)}, bf16[512,1024]{1,0:T(8,128)(2,1)}, u32[]{:S(2)}) copy-start(bf16[512,1024]{1,0:T(8,128)(2,1)} %param.7) | copy-start | bytes 3145732
  7.2 14.4 %copy-start.4 = (bf16[128,256]{1,0:T(8,128)(2,1)S(1)}, bf16[128,256]{1,0:T(8,128)(2,1)}, u32[]{:S(2)}) copy-start(bf16[128,256]{1,0:T(8,128)(2,1)} %param.9) | copy-start | bytes 196612
  7.2 113.7 %all-reduce.8.cloned.1.call-start = ((), (), s32[]{:S(2)}) async-start(), calls=%async_computation | async-start | bytes 524288 | tf_op jit(solution)/shard_map/psum | solution.py:44
  8.4 20.9 %copy-start.1 = (bf16[1024,256]{1,0:T(8,128)(2,1)S(1)}, bf16[1024,256]{1,0:T(8,128)(2,1)}, u32[]{:S(2)}) copy-start(bf16[1024,256]{1,0:T(8,128)(2,1)} %param.11) | copy-start | bytes 1572868
  8.4 23.2 %copy-start.5 = (bf16[128,256]{1,0:T(8,128)(2,1)S(1)}, bf16[128,256]{1,0:T(8,128)(2,1)}, u32[]{:S(2)}) copy-start(bf16[128,256]{1,0:T(8,128)(2,1)} %param.10) | copy-start | bytes 196612
  21.6 11.0 %copy-start.6 = (bf16[256,256]{1,0:T(8,128)(2,1)S(1)}, bf16[256,256]{1,0:T(8,128)(2,1)}, u32[]{:S(2)}) copy-start(bf16[256,256]{1,0:T(8,128)(2,1)} %param.8) | copy-start | bytes 393220
  28.3 231.9 %all-reduce.10.cloned.1.call-start = ((), (), s32[]{:S(2)}) async-start(), calls=%async_computation.1 | async-start | bytes 2621440 | tf_op jit(solution)/shard_map/psum | solution.py:24
  32.5 313.9 %all-reduce.12.cloned.1.call-start = ((), (), s32[]{:S(2)}) async-start(), calls=%async_computation.2 | async-start | bytes 786432 | tf_op jit(solution)/shard_map/psum | solution.py:52
  260.2 86.3 %copy-start.2 = (f32[256,256]{1,0:T(8,128)S(1)}, f32[256,256]{1,0:T(8,128)}, u32[]{:S(2)}) copy-start(f32[256,256]{1,0:T(8,128)} %get-tuple-element.11) | copy-start | bytes 786436
  275.1 135.9 %all-reduce.14.cloned.1.call-start = ((), (), s32[]{:S(2)}) async-start(), calls=%async_computation.3 | async-start | bytes 786432 | tf_op jit(solution)/shard_map/psum | solution.py:56
  346.4 64.6 %copy-start.3 = (f32[256,256]{1,0:T(8,128)S(1)}, f32[256,256]{1,0:T(8,128)}, u32[]{:S(2)}) copy-start(f32[256,256]{1,0:T(8,128)} %get-tuple-element.13) | copy-start | bytes 786436
Sparse Core Ops, SparseCore 0:
  28.4 92.4 all-reduce.7
  126.8 133.3 all-reduce.9
  275.2 71.1 all-reduce.11
  357.4 53.5 all-reduce.13
where the time goes:
time: 420 us
  waiting for transfers between devices  351 us (84%)
  matrix products  28.5 us (7%)
  local copies, waits for them, and re-layouts  18.5 us (4%)
  between operations  13.9 us (3%)
  other arithmetic  7.62 us (2%)
    psum x1, waiting for transfers between devices, on_device(): lax.psum((gram_second, gram_time, gram_column), ('ia', 'ja', 'ka'))  139 us
    psum x1, waiting for transfers between devices, on_device(): slab = lax.psum(slab, ('ja', 'ka'))  88.2 us
    psum x1, waiting for transfers between devices, on_device(): plane_sum, gram_first = lax.psum((plane_sum, gram_first), ('ia', 'ka'))  71.3 us
    psum x1, waiting for transfers between devices, on_device(): time_sum, gram_new = lax.psum((time_sum, gram_new), ('ia', 'ja'))  52.2 us
    unnamed x21, local copies, waits for them, and re-layouts  16.7 us
    unnamed x1, matrix products  11.5 us
  transfers between devices with their start and end apart: 4, of which 4 were waited for; matrix products, arithmetic and copies ran while one was open for 1% of the time, Pallas kernels for 0%

commit v1 on v0

--- a/solution.py
+++ b/solution.py
@@ -41,7 +41,7 @@
     coupled = jnp.dot(matrix, column_factor, preferred_element_type=jnp.float32)
     offset = lax.axis_index("ia") * tile_i
     coupled = lax.psum(coupled, ("ia", "ja", "ka"))
-    slab = lax.psum(slab, ("ja", "ka"))
+    slab = jnp.sum(lax.all_gather(slab, ("ja", "ka")), axis=0)
     numerator = slab + lax.dynamic_slice_in_dim(coupled, offset, tile_i, 0)
     first_new = rescale(first_factor, numerator, gram_total)
     weighted = lax.dot_general(

time: 420 us -> 345 us (0.82)
  waiting for transfers between devices: 351 us -> 269 us
    psum x1 -> x0, waiting for transfers between devices: 88.2 us -> none  [on_device(): slab = lax.psum(slab, ('ja', 'ka'))]
    all_gather x0 -> x1, waiting for transfers between devices: none -> 51.9 us  [on_device(): slab = jnp.sum(lax.all_gather(slab, ('ja', 'ka')), axis=0)]
    psum x1, waiting for transfers between devices: 139 us -> 94.7 us  [on_device(): lax.psum((gram_second, gram_time, gram_column), ('ia', 'ja', 'ka'))]
    unnamed x21 -> x22, local copies, waits for them, and re-layouts: 16.7 us -> 19.7 us
  transfers between devices with their start and end apart: 4 -> 4, of which waited for: 4 -> 4; matrix products, arithmetic and copies ran while one was open for 1% -> 3% of each run, Pallas kernels for 0% -> 0%
where the time goes in v1:
time: 345 us; the launch traced here: 344 us
  waiting for transfers between devices  269 us (78%)
  matrix products  28.3 us (8%)
  local copies, waits for them, and re-layouts  21.7 us (6%)
  between operations  15.8 us (5%)
  other arithmetic  8.68 us (3%)
    psum x1, waiting for transfers between devices, on_device(): lax.psum((gram_second, gram_time, gram_column), ('ia', 'ja', 'ka'))  94.7 us
    psum x1, waiting for transfers between devices, on_device(): plane_sum, gram_first = lax.psum((plane_sum, gram_first), ('ia', 'ka'))  70.3 us
    psum x1, waiting for transfers between devices, on_device(): time_sum, gram_new = lax.psum((time_sum, gram_new), ('ia', 'ja'))  52.4 us
    all_gather x1, waiting for transfers between devices, on_device(): slab = jnp.sum(lax.all_gather(slab, ('ja', 'ka')), axis=0)  51.9 us
    unnamed x22, local copies, waits for them, and re-layouts  19.7 us
    unnamed x1, matrix products  11.5 us
    reduce_sum x1, other arithmetic, on_device(): jnp.sum(weighted * second_new.astype(jnp.float32)[:, None, :], axis=0)  7.66 us
  transfers between devices with their start and end apart: 4, of which 4 were waited for; matrix products, arithmetic and copies ran while one was open for 3% of the time, Pallas kernels for 0%

profile of v1, /device:TPU:0, one launch (start us, length us, event | category | flops | bytes accessed | tf_op | source)
XLA Modules:
  0.0 344.1 jit_solution(9741796041934280777)
XLA Ops:
  8.1 1.0 copy.22
  9.2 13.1 %copy.28 = bf16[256,128,128]{0,2,1:T(8,128)(2,1)} copy(bf16[256,128,128]{2,1,0:T(8,128)(2,1)} %param.6) | data formatting | bytes 16777216 | tf_op args[0]
  22.6 6.5 %fusion.4 = f32[256,256]{0,1:T(8,128)} fusion(bf16[256,128,128]{0,2,1:T(8,128)(2,1)} %copy.28, f32[128,256]{1,0:T(8,128)S(1)} %copy.23, f32[128,256]{1,0:T(8,128)S(1)} %copy.21), kind=kOutput, calls=%fused_computation.13 | convolution fusion | flops 2155872256 | bytes 8912896 | tf_op jit(solution)/shard_map/dot_general | solution.py:38
  29.2 0.9 convolution_select_fusion.3
  30.2 0.9 convolution_select_fusion.2
  31.1 1.0 fusion.15
  32.1 1.2 fusion.14
  33.4 51.9 %all-gather.3.cloned.1.call-done = f32[4096,256]{0,1:T(8,128)} async-done(((f32[256,256]{0,1:T(8,128)}), f32[4096,256]{0,1:T(8,128)}) %all-gather.3.cloned.1.call-update) | async-done | bytes 4194320 | tf_op jit(solution)/shard_map/all_gather | solution.py:44
  85.3 3.9 %copy.36 = f32[32,8,16,256]{3,2,1,0:T(8,128)S(1)} copy(f32[32,8,16,256]{3,1,2,0:T(8,128)} %bitcast.52) | data formatting | bytes 8388608
  89.2 1.0 bitcast_reduce_fusion
  90.4 94.7 %all-reduce.7.cloned.1.call-done = (f32[256,256]{1,0:T(8,128)}, f32[256,256]{1,0:T(8,128)}, f32[256,256]{1,0:T(8,128)}, f32[512,256]{1,0:T(8,128)}) async-done(((f32[256,256]{1,0:T(8,128)}, f32[256,256]{1,0:T(8,128)}, f32[256,256]{1,0:T(8,128)}, f32[512,256]{1,0:T(8,128)}), (f32[256,256]{1,0:T(8,128)}, f32[256,256]{1,0:T(8,128)}, f32[256,256]{1,0:T(8,128)}, ...) | async-done | bytes 1310736 | tf_op jit(solution)/shard_map/psum | solution.py:24
  185.1 1.5 fusion.5
  186.6 0.9 convolution_select_fusion.1
  187.6 11.5 %multiply_reduce_fusion.1 = (f32[128,256]{1,0:T(8,128)S(1)}, f32[256,16384]{0,1}) fusion(f32[128,256]{1,0:T(8,128)S(1)} %copy.23, bf16[256,16384]{0,1:T(8,128)(2,1)} %bitcast.51, bf16[256,256]{1,0:T(8,128)(2,1)S(1)} %fusion.5), kind=kOutput, calls=%fused_computation.1 | convolution fusion | flops 2155839488 | bytes 25559040
  199.1 0.8 copy.29
  200.1 70.3 %all-reduce.9.cloned.1.call-done = (f32[256,256]{1,0:T(8,128)}, f32[128,256]{0,1:T(8,128)}) async-done(((f32[256,256]{1,0:T(8,128)}, f32[128,256]{0,1:T(8,128)}), (f32[256,256]{1,0:T(8,128)}, f32[128,256]{0,1:T(8,128)})) %all-reduce.9.cloned.1.call-update) | async-done | bytes 393232 | tf_op jit(solution)/shard_map/psum | solution.py:52
  270.4 1.4 fusion.9
  271.9 0.9 convolution_select_fusion
  272.9 7.7 %multiply_reduce_fusion = f32[128,256]{1,0:T(8,128)S(1)} fusion(f32[128,128,256]{2,1,0:T(8,128)} %bitcast.50, f32[128,256]{1,0:T(8,128)S(1)} %copy.30), kind=kLoop, calls=%fused_computation | loop fusion | flops 8355840 | bytes 17039360 | tf_op jit(solution)/shard_map/reduce_sum | solution.py:54
  280.5 0.8 copy.31
  281.3 0.7 copy.32
  282.0 52.4 %all-reduce.11.cloned.1.call-done = (f32[256,256]{1,0:T(8,128)}, f32[128,256]{0,1:T(8,128)}) async-done(((f32[256,256]{1,0:T(8,128)}, f32[128,256]{0,1:T(8,128)}), (f32[256,256]{1,0:T(8,128)}, f32[128,256]{0,1:T(8,128)})) %all-reduce.11.cloned.1.call-update) | async-done | bytes 393232 | tf_op jit(solution)/shard_map/psum | solution.py:56
  334.4 1.4 fusion.8
  335.8 0.7 copy.33
  (29 shorter events, 1.0 us)
Async XLA Ops:
  8.0 24.1 %copy-start = (bf16[512,1024]{1,0:T(8,128)(2,1)S(1)}, bf16[512,1024]{1,0:T(8,128)(2,1)}, u32[]{:S(2)}) copy-start(bf16[512,1024]{1,0:T(8,128)(2,1)} %param.7) | copy-start | bytes 3145732
  8.0 77.3 %all-gather.3.cloned.1.call-start = ((), (), s32[]{:S(2)}) async-start(), calls=%async_computation | async-start | bytes 4456448 | tf_op jit(solution)/shard_map/all_gather | solution.py:44
  9.2 13.2 %copy-start.5 = (bf16[128,256]{1,0:T(8,128)(2,1)S(1)}, bf16[128,256]{1,0:T(8,128)(2,1)}, u32[]{:S(2)}) copy-start(bf16[128,256]{1,0:T(8,128)(2,1)} %param.9) | copy-start | bytes 196612
  22.6 7.6 %copy-start.6 = (bf16[128,256]{1,0:T(8,128)(2,1)S(1)}, bf16[128,256]{1,0:T(8,128)(2,1)}, u32[]{:S(2)}) copy-start(bf16[128,256]{1,0:T(8,128)(2,1)} %param.10) | copy-start | bytes 196612
  22.6 8.5 %copy-start.1 = (bf16[1024,256]{1,0:T(8,128)(2,1)S(1)}, bf16[1024,256]{1,0:T(8,128)(2,1)}, u32[]{:S(2)}) copy-start(bf16[1024,256]{1,0:T(8,128)(2,1)} %param.11) | copy-start | bytes 1572868
  29.2 155.9 %all-reduce.7.cloned.1.call-start = ((), (), s32[]{:S(2)}) async-start(), calls=%async_computation.1 | async-start | bytes 2621440 | tf_op jit(solution)/shard_map/psum | solution.py:24
  32.1 153.0 %copy-start.7 = (bf16[256,256]{1,0:T(8,128)(2,1)S(1)}, bf16[256,256]{1,0:T(8,128)(2,1)}, u32[]{:S(2)}) copy-start(bf16[256,256]{1,0:T(8,128)(2,1)} %param.8) | copy-start | bytes 393220
  33.4 237.1 %all-reduce.9.cloned.1.call-start = ((), (), s32[]{:S(2)}) async-start(), calls=%async_computation.2 | async-start | bytes 786432 | tf_op jit(solution)/shard_map/psum | solution.py:52
  186.6 12.5 %copy-start.2 = (bf16[256,256]{1,0:T(8,128)(2,1)}, bf16[256,256]{1,0:T(8,128)(2,1)S(1)}, u32[]{:S(2)}) copy-start(bf16[256,256]{1,0:T(8,128)(2,1)S(1)} %fusion.5) | copy-start | bytes 393220
  187.6 82.9 %copy-start.4 = (f32[256,256]{1,0:T(8,128)S(1)}, f32[256,256]{1,0:T(8,128)}, u32[]{:S(2)}) copy-start(f32[256,256]{1,0:T(8,128)} %get-tuple-element.11) | copy-start | bytes 786436
  199.9 134.5 %all-reduce.11.cloned.1.call-start = ((), (), s32[]{:S(2)}) async-start(), calls=%async_computation.3 | async-start | bytes 786432 | tf_op jit(solution)/shard_map/psum | solution.py:56
  272.9 61.6 %copy-start.3 = (f32[256,256]{1,0:T(8,128)S(1)}, f32[256,256]{1,0:T(8,128)}, u32[]{:S(2)}) copy-start(f32[256,256]{1,0:T(8,128)} %get-tuple-element.13) | copy-start | bytes 786436
Sparse Core Ops, SparseCore 0:
  29.3 55.9 all-gather.2
Sparse Core Ops, SparseCore 1:
  35.5 149.5 all-reduce.6
  199.9 70.4 all-reduce.8
  281.4 53.0 all-reduce.10
